TPU v7x, 512 devices: a whole 4x4x16 slice. The times are simulated.
512 devices in a mesh: section: 16 (over z), chan: 32 (over y, x, core).
Axes of the slice: x: 4, y: 4, z: 16, core: 2. Of those that a mesh axis runs over, the one named last changes fastest.
Arguments:
- inputs: bfloat16 [4, 512, 256], P(None, 'chan'), may hold values from -6 to 6
- front: bfloat16 [16, 512, 256], P('section', 'chan'), may hold values from -6 to 6
- back: bfloat16 [16, 512, 256], P('section', 'chan'), may hold values from -6 to 6
- saved: bfloat16 [16, 4, 512, 256], P('section', None, 'chan'), may hold values from -6 to 6
- weights: bfloat16 [16, 512, 27, 512], P('section', 'chan'), may hold values from -0.1875 to 0.1875
- cotangent: bfloat16 [4, 512, 256], P(None, 'chan'), may hold values from -6 to 6
Outputs:
- acts: bfloat16 [16, 4, 512, 256], P('section', None, 'chan')
- grads: bfloat16 [16, 4, 512, 256], P('section', None, 'chan')
- weight_grads: float32 [16, 512, 27, 512], P('section', 'chan')
All inputs are finite; a program needn't handle non-finite values.
Results may differ from a plain program's by a relative error of at most 0.035.
Values may be sent and summed in bfloat16 or wider, within the bound.
No kernel may reach another device: no remote copies, remote signals or barrier semaphores. Data moves between devices by JAX's collectives and lax.ppermute only.
A program may use at most 128 MiB of HBM per device.

v0:
```python
import jax
import jax.numpy as jnp
from jax import lax
from jax.sharding import PartitionSpec as P

SX = 4
SY = 8
SZ = 8
TAP_OFFSETS = [(i - 1, j - 1, l - 1) for i in range(3) for j in range(3) for l in range(3)]


def from_behind(value, axis, steps):
    count = lax.axis_size(axis)
    first, last = (max(0, -steps), min(count, count - steps))
    return lax.ppermute(value, axis, [(source, source + steps) for source in range(first, last)])


def shifted_view(values, offset):
    cell_count = SX * SY * SZ
    margin = SY * SZ + SZ + 1
    lead = values.ndim - 1
    padded = jnp.pad(values, [(0, 0)] * lead + [(margin, margin)])
    delta = offset[0] * SY * SZ + offset[1] * SZ + offset[2]
    moved = padded[..., margin + delta : margin + delta + cell_count]
    index = jnp.arange(cell_count, dtype=jnp.int32)
    first_pos = index // (SY * SZ) + offset[0]
    second_pos = index // SZ % SY + offset[1]
    third_pos = index % SZ + offset[2]
    inside = (
        (first_pos >= 0)
        & (first_pos < SX)
        & (second_pos >= 0)
        & (second_pos < SY)
        & (third_pos >= 0)
        & (third_pos < SZ)
    )
    return jnp.where(inside, moved, jnp.zeros_like(moved))


def tap_sum(taps):
    accum = shifted_view(taps[..., 0, :], TAP_OFFSETS[0])
    for index in range(1, 27):
        accum = accum + shifted_view(taps[..., index, :], TAP_OFFSETS[index])
    return accum


def tap_spread(values):
    return jnp.stack([shifted_view(values, (-o[0], -o[1], -o[2])) for o in TAP_OFFSETS], axis=-2)


def silu_slope(pre):
    logistic = jax.nn.sigmoid(pre)
    return logistic * (1.0 + pre * (1.0 - logistic))


def body(inputs, front, back, saved, weights, cotangent):
    section_count = lax.axis_size("section")
    section_index = lax.axis_index("section")
    first_section = section_index == 0
    last_section = section_index == section_count - 1
    round_count, own_filters, cell_count = inputs.shape
    channels = weights.shape[3]
    weight_rows = weights.reshape(own_filters * 27, channels)
    acts_list = []
    grads_list = []
    filter_grad = jnp.zeros((own_filters * 27, channels), jnp.float32)
    forward_recv = front[0]
    backward_recv = back[0]
    for round_index in range(round_count):
        layer_in = jnp.where(first_section, inputs[round_index], forward_recv)
        taps = jnp.dot(
            weight_rows,
            lax.all_gather(layer_in, "chan", axis=0, tiled=True),
            preferred_element_type=jnp.float32,
        )
        pre = tap_sum(taps.reshape(own_filters, 27, cell_count))
        layer_out = jax.nn.silu(pre).astype(jnp.bfloat16)
        acts_list.append(layer_out)
        if round_index + 1 < round_count:
            forward_recv = from_behind(layer_out, "section", 1)
        whole_in = lax.all_gather(saved[0, round_index], "chan", axis=0, tiled=True)
        back_taps = jnp.dot(weight_rows, whole_in, preferred_element_type=jnp.float32)
        pre_back = tap_sum(back_taps.reshape(own_filters, 27, cell_count))
        grad_out = jnp.where(last_section, cotangent[round_index], backward_recv)
        dpre = (grad_out.astype(jnp.float32) * silu_slope(pre_back)).astype(jnp.bfloat16)
        spread = tap_spread(dpre).reshape(own_filters * 27, cell_count)
        grad_in = lax.psum_scatter(
            lax.dot_general(
                weight_rows, spread, (((0,), (0,)), ((), ())), preferred_element_type=jnp.float32
            ).astype(jnp.bfloat16),
            "chan",
            scatter_dimension=0,
            tiled=True,
        )
        filter_grad = filter_grad + lax.dot_general(
            spread, whole_in, (((1,), (1,)), ((), ())), preferred_element_type=jnp.float32
        )
        grads_list.append(grad_in)
        if round_index + 1 < round_count:
            backward_recv = from_behind(grad_in, "section", -1)
    acts = jnp.stack(acts_list, axis=0)[None]
    grads = jnp.stack(grads_list, axis=0)[None]
    return (acts, grads, filter_grad.reshape(1, own_filters, 27, channels))


def solution(mesh):
    return jax.shard_map(
        body,
        mesh=mesh,
        in_specs=(
            P(None, "chan", None),
            P("section", "chan", None),
            P("section", "chan", None),
            P("section", None, "chan", None),
            P("section", "chan", None, None),
            P(None, "chan", None),
        ),
        out_specs=(
            P("section", None, "chan", None),
            P("section", None, "chan", None),
            P("section", "chan", None, None),
        ),
        check_vma=False,
    )
```

profile of v0, /device:TPU:2, one launch (start us, length us, event | category | flops | bytes accessed | tf_op | source)
XLA Modules:
  0.0 543.6 jit_solution(12856307479175917620)
XLA Ops:
  7.2 0.8 fusion.670
  8.0 27.6 %all-gather.1 = bf16[1,1,512,256]{3,2,1,0:T(8,128)(2,1)S(1)} all-gather(bf16[1,1,16,256]{3,2,1,0:T(8,128)(2,1)S(1)} %get-tuple-element.222), channel_id=3, replica_groups=mesh['section'=16,'chan'=32] {'chan'}, dimensions={2}, use_global_device_ids=true | all-gather | bytes 270336 | tf_op jit(solution)/shard_map/all_gather | solution.py:81
  35.6 1.5 fusion.4
  39.2 0.9 fusion.443
  42.5 1.1 fusion
  44.3 22.0 %all-gather = bf16[1,512,256]{2,1,0:T(8,128)(2,1)S(1)} all-gather(bf16[1,16,256]{2,1,0:T(8,128)(2,1)S(1)} %slice_select_fusion), channel_id=2, replica_groups=mesh['section'=16,'chan'=32] {'chan'}, dimensions={1}, use_global_device_ids=true | all-gather | bytes 270336 | tf_op jit(solution)/shard_map/all_gather | solution.py:73
  67.6 2.0 collective-permute-start
  69.6 23.9 %all-gather.2 = bf16[1,1,512,256]{3,2,1,0:T(8,128)(2,1)S(1)} all-gather(bf16[1,1,16,256]{3,2,1,0:T(8,128)(2,1)S(1)} %get-tuple-element.223), channel_id=4, replica_groups=mesh['section'=16,'chan'=32] {'chan'}, dimensions={2}, use_global_device_ids=true | all-gather | bytes 270336 | tf_op jit(solution)/shard_map/all_gather | solution.py:81
  93.8 0.9 slice_bitcast_fusion.80
  95.7 22.7 %all-gather.3 = bf16[1,1,512,256]{3,2,1,0:T(8,128)(2,1)S(1)} all-gather(bf16[1,1,16,256]{3,2,1,0:T(8,128)(2,1)S(1)} %get-tuple-element.225), channel_id=5, replica_groups=mesh['section'=16,'chan'=32] {'chan'}, dimensions={2}, use_global_device_ids=true | all-gather | bytes 270336 | tf_op jit(solution)/shard_map/all_gather | solution.py:81
  118.7 0.9 slice_bitcast_fusion.53
  119.5 24.2 %all-gather.4 = bf16[1,1,512,256]{3,2,1,0:T(8,128)(2,1)S(1)} all-gather(bf16[1,1,16,256]{3,2,1,0:T(8,128)(2,1)S(1)} %get-tuple-element.224), channel_id=6, replica_groups=mesh['section'=16,'chan'=32] {'chan'}, dimensions={2}, use_global_device_ids=true | all-gather | bytes 270336 | tf_op jit(solution)/shard_map/all_gather | solution.py:81
  144.0 0.9 slice_bitcast_fusion.26
  145.5 22.6 %all_gather.25 = bf16[512,256]{1,0:T(8,128)(2,1)S(1)} all-gather(bf16[16,256]{1,0:T(8,128)(2,1)S(1)} %bitcast_select_fusion.5), channel_id=1, replica_groups=mesh['section'=16,'chan'=32] {'chan'}, dimensions={0}, use_global_device_ids=true | all-gather | bytes 270336 | tf_op jit(solution)/shard_map/all_gather | solution.py:73
  170.2 3.8 collective-permute-start.1
  176.1 23.8 %all_gather.26 = bf16[512,256]{1,0:T(8,128)(2,1)S(1)} all-gather(bf16[16,256]{1,0:T(8,128)(2,1)S(1)} %bitcast_select_fusion.4), channel_id=1, replica_groups=mesh['section'=16,'chan'=32] {'chan'}, dimensions={0}, use_global_device_ids=true | all-gather | bytes 270336 | tf_op jit(solution)/shard_map/all_gather | solution.py:73
  200.9 1.3 collective-permute-start.3
  202.7 4.8 collective-permute-start.2
  208.3 0.9 multiply_convert_fusion.2
  211.4 1.1 fusion.1
  212.5 0.7 bitcast_select_fusion.3
  213.3 22.7 %all_gather.27 = bf16[512,256]{1,0:T(8,128)(2,1)S(1)} all-gather(bf16[16,256]{1,0:T(8,128)(2,1)S(1)} %bitcast_select_fusion.3), channel_id=1, replica_groups=mesh['section'=16,'chan'=32] {'chan'}, dimensions={0}, use_global_device_ids=true | all-gather | bytes 270336 | tf_op jit(solution)/shard_map/all_gather | solution.py:73
  236.3 78.7 %reduce-scatter.7.cloned.1.call-done = bf16[16,256]{1,0:T(8,128)(2,1)} async-done(((bf16[512,256]{1,0:T(8,128)(2,1)}), bf16[16,256]{1,0:T(8,128)(2,1)}) %reduce-scatter.7.cloned.1.call-update) | async-done | bytes 8208 | tf_op jit(solution)/shard_map/reduce_scatter | solution.py:87
  315.1 1.5 collective-permute-start.4
  316.9 0.9 fusion.662
  317.8 3.0 collective-permute-done.4
  321.6 1.1 multiply_convert_fusion.1
  324.9 1.1 fusion.2
  326.7 0.7 copy-done.72
  327.4 0.7 copy-done.71
  328.2 0.7 copy-done.70
  328.9 0.7 copy-done.69
  329.6 0.7 copy-done.68
  330.3 0.7 copy-done.67
  331.0 0.7 copy-done.66
  331.7 0.7 copy-done.65
  332.5 0.7 copy-done.64
  333.2 0.7 copy-done.63
  333.9 0.7 copy-done.62
  334.6 0.7 copy-done.61
  336.8 88.7 %reduce-scatter.9.cloned.1.call-done = bf16[16,256]{1,0:T(8,128)(2,1)} async-done(((bf16[512,256]{1,0:T(8,128)(2,1)}), bf16[16,256]{1,0:T(8,128)(2,1)}) %reduce-scatter.9.cloned.1.call-update) | async-done | bytes 8208 | tf_op jit(solution)/shard_map/reduce_scatter | solution.py:87
  425.5 1.3 collective-permute-start.5
  427.4 3.9 collective-permute-done.5
  432.0 0.9 multiply_convert_fusion
  435.2 1.1 fusion.3
  437.0 1.4 copy.461
  438.5 97.3 %reduce-scatter.11.cloned.1.call-done = bf16[16,256]{1,0:T(8,128)(2,1)} async-done(((bf16[512,256]{1,0:T(8,128)(2,1)}), bf16[16,256]{1,0:T(8,128)(2,1)}) %reduce-scatter.11.cloned.1.call-update) | async-done | bytes 8208 | tf_op jit(solution)/shard_map/reduce_scatter | solution.py:87
  535.8 1.3 maximum_bitcast_fusion.1
  (591 shorter events, 24.9 us)
Async XLA Ops:
  7.2 193.7 %reduce-scatter.5.cloned.1.call-start = ((), (), s32[]{:S(2)}) async-start(), calls=%async_computation.4 | async-start | bytes 270336 | tf_op jit(solution)/shard_map/reduce_scatter | solution.py:87
  37.4 29.8 %copy-start.55 = (pred[256]{0:T(512)(128)(4,1)}, pred[256]{0:T(512)(128)(4,1)S(1)}, u32[]{:S(2)}) copy-start(pred[256]{0:T(512)(128)(4,1)S(1)} %get-tuple-element.253) | copy-start | bytes 772
  37.4 29.8 %copy-start.58 = (pred[256]{0:T(512)(128)(4,1)}, pred[256]{0:T(512)(128)(4,1)S(1)}, u32[]{:S(2)}) copy-start(pred[256]{0:T(512)(128)(4,1)S(1)} %get-tuple-element.252) | copy-start | bytes 772
  37.5 29.8 %copy-start.49 = (pred[256]{0:T(512)(128)(4,1)}, pred[256]{0:T(512)(128)(4,1)S(1)}, u32[]{:S(2)}) copy-start(pred[256]{0:T(512)(128)(4,1)S(1)} %get-tuple-element.255) | copy-start | bytes 772
  37.5 29.8 %copy-start.52 = (pred[256]{0:T(512)(128)(4,1)}, pred[256]{0:T(512)(128)(4,1)S(1)}, u32[]{:S(2)}) copy-start(pred[256]{0:T(512)(128)(4,1)S(1)} %get-tuple-element.254) | copy-start | bytes 772
  37.5 29.7 %copy-start.43 = (pred[256]{0:T(512)(128)(4,1)}, pred[256]{0:T(512)(128)(4,1)S(1)}, u32[]{:S(2)}) copy-start(pred[256]{0:T(512)(128)(4,1)S(1)} %get-tuple-element.257) | copy-start | bytes 772
  37.5 29.7 %copy-start.46 = (pred[256]{0:T(512)(128)(4,1)}, pred[256]{0:T(512)(128)(4,1)S(1)}, u32[]{:S(2)}) copy-start(pred[256]{0:T(512)(128)(4,1)S(1)} %get-tuple-element.256) | copy-start | bytes 772
  37.5 29.7 %copy-start.37 = (pred[256]{0:T(512)(128)(4,1)}, pred[256]{0:T(512)(128)(4,1)S(1)}, u32[]{:S(2)}) copy-start(pred[256]{0:T(512)(128)(4,1)S(1)} %get-tuple-element.259) | copy-start | bytes 772
  37.5 29.7 %copy-start.40 = (pred[256]{0:T(512)(128)(4,1)}, pred[256]{0:T(512)(128)(4,1)S(1)}, u32[]{:S(2)}) copy-start(pred[256]{0:T(512)(128)(4,1)S(1)} %get-tuple-element.258) | copy-start | bytes 772
  37.6 29.7 %copy-start.31 = (pred[256]{0:T(512)(128)(4,1)}, pred[256]{0:T(512)(128)(4,1)S(1)}, u32[]{:S(2)}) copy-start(pred[256]{0:T(512)(128)(4,1)S(1)} %get-tuple-element.261) | copy-start | bytes 772
  37.6 29.7 %copy-start.34 = (pred[256]{0:T(512)(128)(4,1)}, pred[256]{0:T(512)(128)(4,1)S(1)}, u32[]{:S(2)}) copy-start(pred[256]{0:T(512)(128)(4,1)S(1)} %get-tuple-element.260) | copy-start | bytes 772
  37.6 29.7 %copy-start.25 = (pred[256]{0:T(512)(128)(4,1)}, pred[256]{0:T(512)(128)(4,1)S(1)}, u32[]{:S(2)}) copy-start(pred[256]{0:T(512)(128)(4,1)S(1)} %get-tuple-element.263) | copy-start | bytes 772
  37.6 29.7 %copy-start.28 = (pred[256]{0:T(512)(128)(4,1)}, pred[256]{0:T(512)(128)(4,1)S(1)}, u32[]{:S(2)}) copy-start(pred[256]{0:T(512)(128)(4,1)S(1)} %get-tuple-element.262) | copy-start | bytes 772
  37.6 29.7 %copy-start.19 = (pred[256]{0:T(512)(128)(4,1)}, pred[256]{0:T(512)(128)(4,1)S(1)}, u32[]{:S(2)}) copy-start(pred[256]{0:T(512)(128)(4,1)S(1)} %get-tuple-element.265) | copy-start | bytes 772
  37.7 29.7 %copy-start.22 = (pred[256]{0:T(512)(128)(4,1)}, pred[256]{0:T(512)(128)(4,1)S(1)}, u32[]{:S(2)}) copy-start(pred[256]{0:T(512)(128)(4,1)S(1)} %get-tuple-element.264) | copy-start | bytes 772
  37.7 29.7 %copy-start.13 = (pred[256]{0:T(512)(128)(4,1)}, pred[256]{0:T(512)(128)(4,1)S(1)}, u32[]{:S(2)}) copy-start(pred[256]{0:T(512)(128)(4,1)S(1)} %get-tuple-element.267) | copy-start | bytes 772
  37.7 29.7 %copy-start.16 = (pred[256]{0:T(512)(128)(4,1)}, pred[256]{0:T(512)(128)(4,1)S(1)}, u32[]{:S(2)}) copy-start(pred[256]{0:T(512)(128)(4,1)S(1)} %get-tuple-element.266) | copy-start | bytes 772
  37.7 29.6 %copy-start.7 = (pred[256]{0:T(512)(128)(4,1)}, pred[256]{0:T(512)(128)(4,1)S(1)}, u32[]{:S(2)}) copy-start(pred[256]{0:T(512)(128)(4,1)S(1)} %get-tuple-element.269) | copy-start | bytes 772
  37.7 29.6 %copy-start.10 = (pred[256]{0:T(512)(128)(4,1)}, pred[256]{0:T(512)(128)(4,1)S(1)}, u32[]{:S(2)}) copy-start(pred[256]{0:T(512)(128)(4,1)S(1)} %get-tuple-element.268) | copy-start | bytes 772
  37.8 29.6 %copy-start.4 = (pred[256]{0:T(512)(128)(4,1)}, pred[256]{0:T(512)(128)(4,1)S(1)}, u32[]{:S(2)}) copy-start(pred[256]{0:T(512)(128)(4,1)S(1)} %get-tuple-element.270) | copy-start | bytes 772
  43.6 271.5 %reduce-scatter.7.cloned.1.call-start = ((), (), s32[]{:S(2)}) async-start(), calls=%async_computation.5 | async-start | bytes 270336 | tf_op jit(solution)/shard_map/reduce_scatter | solution.py:87
  67.6 25.9 %copy-start.147 = (bf16[16,256]{1,0:T(8,128)(2,1)}, bf16[16,256]{1,0:T(8,128)(2,1)S(1)}, u32[]{:S(2)}) copy-start(bf16[16,256]{1,0:T(8,128)(2,1)S(1)} %multiply_convert_fusion.6) | copy-start | bytes 24580
  67.6 77.9 %collective-permute-start = (bf16[16,256]{1,0:T(8,128)(2,1)S(1)}, bf16[16,256]{1,0:T(8,128)(2,1)S(1)}, u32[]{:S(2)}, u32[]{:S(2)}) collective-permute-start(bf16[16,256]{1,0:T(8,128)(2,1)S(1)} %multiply_convert_fusion.6), channel_id=1, source_target_pairs={{0,32},{32,64},{64,96},{96,128},{128,160},{160,192},{192,224},{224... | collective-permute-start | bytes 24584 | tf_op jit(solution)/shard_map/ppermute | solution.py:15
  118.7 26.2 %copy-start.2 = (f32[16,27,256]{2,0,1:T(8,128)}, f32[16,27,256]{2,0,1:T(8,128)S(1)}, u32[]{:S(2)}) copy-start(f32[16,27,256]{2,0,1:T(8,128)S(1)} %fusion.8) | copy-start | bytes 1327108
  144.0 30.0 %copy-start.1 = (f32[16,27,256]{2,0,1:T(8,128)}, f32[16,27,256]{2,0,1:T(8,128)S(1)}, u32[]{:S(2)}) copy-start(f32[16,27,256]{2,0,1:T(8,128)S(1)} %fusion.6) | copy-start | bytes 1327108
  170.2 5.2 collective-permute-start.1
  200.9 6.6 %collective-permute-start.3 = (bf16[16,256]{1,0:T(8,128)(2,1)}, bf16[16,256]{1,0:T(8,128)(2,1)S(1)}, u32[]{:S(2)}, u32[]{:S(2)}) collective-permute-start(bf16[16,256]{1,0:T(8,128)(2,1)} %reduce-scatter.5.cloned.1.call-done), channel_id=1, source_target_pairs={{32,0},{64,32},{96,64},{128,96},{160,128},{192,160},{224,192},{256... | collective-permute-start | bytes 24584 | tf_op jit(solution)/shard_map/ppermute | solution.py:15
  202.2 5.3 copy-start.91
  202.2 5.3 copy-start.92
  202.2 5.3 copy-start.93
  202.2 5.3 copy-start.94
  202.2 5.3 copy-start.128
  202.3 5.3 copy-start.129
  202.3 5.3 copy-start.130
  202.3 5.3 copy-start.131
  202.3 5.3 copy-start.132
  202.3 5.3 copy-start.133
  202.3 5.3 copy-start.134
  202.3 5.3 copy-start.135
  202.3 5.3 copy-start.136
  202.7 9.9 %collective-permute-start.2 = (bf16[16,256]{1,0:T(8,128)(2,1)S(1)}, bf16[16,256]{1,0:T(8,128)(2,1)S(1)}, u32[]{:S(2)}, u32[]{:S(2)}) collective-permute-start(bf16[16,256]{1,0:T(8,128)(2,1)S(1)} %multiply_convert_fusion.4), channel_id=1, source_target_pairs={{0,32},{32,64},{64,96},{96,128},{128,160},{160,192},{192,224},{224... | collective-permute-start | bytes 24584 | tf_op jit(solution)/shard_map/ppermute | solution.py:15
  212.5 213.0 %reduce-scatter.9.cloned.1.call-start = ((), (), s32[]{:S(2)}) async-start(), calls=%async_computation.6 | async-start | bytes 270336 | tf_op jit(solution)/shard_map/reduce_scatter | solution.py:87
  315.1 5.7 %collective-permute-start.4 = (bf16[16,256]{1,0:T(8,128)(2,1)}, bf16[16,256]{1,0:T(8,128)(2,1)S(1)}, u32[]{:S(2)}, u32[]{:S(2)}) collective-permute-start(bf16[16,256]{1,0:T(8,128)(2,1)} %reduce-scatter.7.cloned.1.call-done), channel_id=1, source_target_pairs={{32,0},{64,32},{96,64},{128,96},{160,128},{192,160},{224,192},{256... | collective-permute-start | bytes 24584 | tf_op jit(solution)/shard_map/ppermute | solution.py:15
  326.0 209.8 %reduce-scatter.11.cloned.1.call-start = ((), (), s32[]{:S(2)}) async-start(), calls=%async_computation.7 | async-start | bytes 270336 | tf_op jit(solution)/shard_map/reduce_scatter | solution.py:87
  425.5 5.7 %collective-permute-start.5 = (bf16[16,256]{1,0:T(8,128)(2,1)}, bf16[16,256]{1,0:T(8,128)(2,1)S(1)}, u32[]{:S(2)}, u32[]{:S(2)}) collective-permute-start(bf16[16,256]{1,0:T(8,128)(2,1)} %reduce-scatter.9.cloned.1.call-done), channel_id=1, source_target_pairs={{32,0},{64,32},{96,64},{128,96},{160,128},{192,160},{224,192},{256... | collective-permute-start | bytes 24584 | tf_op jit(solution)/shard_map/ppermute | solution.py:15
  437.0 98.8 %copy-start.156 = (bf16[16,256]{1,0:T(8,128)(2,1)S(1)}, bf16[16,256]{1,0:T(8,128)(2,1)}, u32[]{:S(2)}) copy-start(bf16[16,256]{1,0:T(8,128)(2,1)} %reduce-scatter.5.cloned.1.call-done) | copy-start | bytes 24580
  437.0 98.8 %copy-start.157 = (bf16[16,256]{1,0:T(8,128)(2,1)S(1)}, bf16[16,256]{1,0:T(8,128)(2,1)}, u32[]{:S(2)}) copy-start(bf16[16,256]{1,0:T(8,128)(2,1)} %reduce-scatter.7.cloned.1.call-done) | copy-start | bytes 24580
  437.0 98.8 %copy-start.158 = (bf16[16,256]{1,0:T(8,128)(2,1)S(1)}, bf16[16,256]{1,0:T(8,128)(2,1)}, u32[]{:S(2)}) copy-start(bf16[16,256]{1,0:T(8,128)(2,1)} %reduce-scatter.9.cloned.1.call-done) | copy-start | bytes 24580
  (121 other events, 350.5 us)
Sparse Core Ops, SparseCore 0:
  43.7 99.4 reduce-scatter.4
  212.6 102.4 reduce-scatter.6
  326.1 99.3 reduce-scatter.8
  436.4 99.3 reduce-scatter.10
where the time goes:
time: 547 us; the launch traced here: 544 us
  waiting for transfers between devices  272 us (50%)
  blocking collectives  190 us (35%)
  local copies, waits for them, and re-layouts  24.7 us (5%)
  between operations  17 us (3%)
  other arithmetic  16.3 us (3%)
  starting transfers between devices  14.9 us (3%)
  matrix products  8.87 us (2%)
    reduce_scatter x4, waiting for transfers between devices, body(): lax.psum_scatter(lax.dot_general(weight_rows, spread, (((0,), (0,)), ((),...  265 us
    all_gather x4, blocking collectives, body(): whole_in = lax.all_gather(saved[0, round_index], 'chan', axis=0, tiled=True)  98.4 us
    all_gather x4, blocking collectives, body(): lax.all_gather(layer_in, 'chan', axis=0, tiled=True)  91.1 us
    unnamed x398, local copies, waits for them, and re-layouts  15.7 us
    ppermute x6, starting transfers between devices, from_behind(): lax.ppermute(value, axis, [(source, source + steps) for source in range(f...  14.7 us
  transfers between devices with their start and end apart: 10, of which 6 were waited for; matrix products, arithmetic and copies ran while one was open for 3% of the time, Pallas kernels for 0%

commit v1 on v0

--- a/solution.py
+++ b/solution.py
@@ -78,7 +78,12 @@
         acts_list.append(layer_out)
         if round_index + 1 < round_count:
             forward_recv = from_behind(layer_out, "section", 1)
-        whole_in = lax.all_gather(saved[0, round_index], "chan", axis=0, tiled=True)
+        whole_in = jnp.concatenate(
+            lax.all_to_all(
+                jnp.stack([saved[0, round_index]] * lax.axis_size("chan")), "chan", 0, 0
+            ),
+            axis=0,
+        )
         back_taps = jnp.dot(weight_rows, whole_in, preferred_element_type=jnp.float32)
         pre_back = tap_sum(back_taps.reshape(own_filters, 27, cell_count))
         grad_out = jnp.where(last_section, cotangent[round_index], backward_recv)

time: 547 us -> 600 us (1.097)
  waiting for transfers between devices: 272 us -> 414 us
  blocking collectives: 190 us -> 98.7 us
  starting transfers between devices: 14.9 us -> 35 us
  local copies, waits for them, and re-layouts: 24.7 us -> 13.8 us
    reduce_scatter x4, waiting for transfers between devices: 265 us -> 383 us  [body(): lax.psum_scatter(lax.dot_general(weight_rows, spread, (((0,), (0,)), ((),...]
    all_gather x4 -> x0, blocking collectives: 98.4 us -> none  [body(): whole_in = lax.all_gather(saved[0, round_index], 'chan', axis=0, tiled=True)]
    all_to_all x0 -> x4, starting transfers between devices: none -> 21.3 us  [body(): lax.all_to_all(jnp.stack([saved[0, round_index]] * lax.axis_size('chan'))...]
    all_to_all x0 -> x4, waiting for transfers between devices: none -> 16 us  [body(): lax.all_to_all(jnp.stack([saved[0, round_index]] * lax.axis_size('chan'))...]
    unnamed x398 -> x186, local copies, waits for them, and re-layouts: 15.7 us -> 5.75 us
    ppermute x6, waiting for transfers between devices: 7.58 us -> 15.4 us  [from_behind(): lax.ppermute(value, axis, [(source, source + steps) for source in range(f...]
    all_gather x4, blocking collectives: 91.1 us -> 98.7 us  [body(): lax.all_gather(layer_in, 'chan', axis=0, tiled=True)]
  transfers between devices with their start and end apart: 10 -> 14, of which waited for: 6 -> 12; matrix products, arithmetic and copies ran while one was open for 3% -> 2% of each run, Pallas kernels for 0% -> 0%
where the time goes in v1:
time: 600 us; the launch traced here: 599 us
  waiting for transfers between devices  414 us (69%)
  blocking collectives  98.7 us (16%)
  starting transfers between devices  35 us (6%)
  between operations  15.9 us (3%)
  local copies, waits for them, and re-layouts  13.8 us (2%)
  other arithmetic  13.3 us (2%)
  matrix products  7.89 us (1%)
    reduce_scatter x4, waiting for transfers between devices, body(): lax.psum_scatter(lax.dot_general(weight_rows, spread, (((0,), (0,)), ((),...  383 us
    all_gather x4, blocking collectives, body(): lax.all_gather(layer_in, 'chan', axis=0, tiled=True)  98.7 us
    all_to_all x4, starting transfers between devices, body(): lax.all_to_all(jnp.stack([saved[0, round_index]] * lax.axis_size('chan'))...  21.3 us
    all_to_all x4, waiting for transfers between devices, body(): lax.all_to_all(jnp.stack([saved[0, round_index]] * lax.axis_size('chan'))...  16 us
    ppermute x6, waiting for transfers between devices, from_behind(): lax.ppermute(value, axis, [(source, source + steps) for source in range(f...  15.4 us
    ppermute x6, starting transfers between devices, from_behind(): lax.ppermute(value, axis, [(source, source + steps) for source in range(f...  13.5 us
  transfers between devices with their start and end apart: 14, of which 12 were waited for; matrix products, arithmetic and copies ran while one was open for 2% of the time, Pallas kernels for 0%

profile of v1, /device:TPU:2, one launch (start us, length us, event | category | flops | bytes accessed | tf_op | source)
XLA Modules:
  0.0 598.9 jit_solution(17991581174404390956)
XLA Ops:
  7.4 1.3 copy.233
  8.8 0.6 copy-done.46
  9.4 27.6 %all-gather = bf16[1,512,256]{2,1,0:T(8,128)(2,1)S(1)} all-gather(bf16[1,16,256]{2,1,0:T(8,128)(2,1)S(1)} %slice_select_fusion), channel_id=2, replica_groups=mesh['section'=16,'chan'=32] {'chan'}, dimensions={1}, use_global_device_ids=true | all-gather | bytes 270336 | tf_op jit(solution)/shard_map/all_gather | solution.py:73
  38.1 1.3 collective-permute-start
  39.4 1.3 collective-permute-done
  40.8 22.8 %all_gather.13 = bf16[512,256]{1,0:T(8,128)(2,1)S(1)} all-gather(bf16[16,256]{1,0:T(8,128)(2,1)S(1)} %bitcast_select_fusion.5), channel_id=1, replica_groups=mesh['section'=16,'chan'=32] {'chan'}, dimensions={0}, use_global_device_ids=true | all-gather | bytes 270336 | tf_op jit(solution)/shard_map/all_gather | solution.py:73
  64.8 4.2 collective-permute-start.1
  69.0 1.3 collective-permute-done.1
  70.4 23.9 %all_gather.14 = bf16[512,256]{1,0:T(8,128)(2,1)S(1)} all-gather(bf16[16,256]{1,0:T(8,128)(2,1)S(1)} %bitcast_select_fusion.4), channel_id=1, replica_groups=mesh['section'=16,'chan'=32] {'chan'}, dimensions={0}, use_global_device_ids=true | all-gather | bytes 270336 | tf_op jit(solution)/shard_map/all_gather | solution.py:73
  95.5 4.2 collective-permute-start.2
  99.7 0.7 stack.383
  100.4 5.6 all-to-all-start
  106.0 24.5 %all_gather.15 = bf16[512,256]{1,0:T(8,128)(2,1)S(1)} all-gather(bf16[16,256]{1,0:T(8,128)(2,1)S(1)} %bitcast_select_fusion.3), channel_id=1, replica_groups=mesh['section'=16,'chan'=32] {'chan'}, dimensions={0}, use_global_device_ids=true | all-gather | bytes 270336 | tf_op jit(solution)/shard_map/all_gather | solution.py:73
  131.8 0.6 maximum_bitcast_fusion
  132.4 0.7 stack.413
  133.1 5.8 all-to-all-start.1
  138.9 0.4 fusion.4
  139.9 0.7 copy-done.48
  140.6 0.9 fusion.431
  143.7 2.9 all-to-all-done.1
  146.6 0.7 stack.443
  147.3 5.0 all-to-all-start.2
  152.4 1.1 fusion
  153.8 6.4 %all-to-all-done.2 = bf16[32,16,256]{2,1,0:T(8,128)(2,1)S(1)} async-done(((bf16[32,16,256]{2,1,0:T(8,128)(2,1)}), bf16[32,16,256]{2,1,0:T(8,128)(2,1)S(1)}, u32[]{:S(2)}, u32[]{:S(2)}) %all-to-all-start.2) | async-done | bytes 262176 | tf_op jit(solution)/shard_map/all_to_all | solution.py:82
  160.1 0.7 stack.473
  160.8 5.0 all-to-all-start.3
  166.1 0.7 slice_bitcast_fusion.80
  166.8 6.8 %all-to-all-done.3 = bf16[32,16,256]{2,1,0:T(8,128)(2,1)S(1)} async-done(((bf16[32,16,256]{2,1,0:T(8,128)(2,1)}), bf16[32,16,256]{2,1,0:T(8,128)(2,1)S(1)}, u32[]{:S(2)}, u32[]{:S(2)}) %all-to-all-start.3) | async-done | bytes 262176 | tf_op jit(solution)/shard_map/all_to_all | solution.py:82
  173.9 88.4 %reduce-scatter.5.cloned.1.call-done = bf16[16,256]{1,0:T(8,128)(2,1)} async-done(((bf16[512,256]{1,0:T(8,128)(2,1)}), bf16[16,256]{1,0:T(8,128)(2,1)}) %reduce-scatter.5.cloned.1.call-update) | async-done | bytes 8208 | tf_op jit(solution)/shard_map/reduce_scatter | solution.py:92
  262.3 1.3 collective-permute-start.3
  263.8 4.3 collective-permute-done.3
  268.2 0.6 copy-done.32
  271.2 1.1 fusion.1
  272.4 0.7 slice_bitcast_fusion.26
  273.2 98.8 %reduce-scatter.7.cloned.1.call-done = bf16[16,256]{1,0:T(8,128)(2,1)} async-done(((bf16[512,256]{1,0:T(8,128)(2,1)}), bf16[16,256]{1,0:T(8,128)(2,1)}) %reduce-scatter.7.cloned.1.call-update) | async-done | bytes 8208 | tf_op jit(solution)/shard_map/reduce_scatter | solution.py:92
  372.0 1.3 collective-permute-start.4
  373.3 4.4 collective-permute-done.4
  380.1 1.1 fusion.2
  381.3 0.6 slice_bitcast_fusion.25
  382.5 98.3 %reduce-scatter.9.cloned.1.call-done = bf16[16,256]{1,0:T(8,128)(2,1)} async-done(((bf16[512,256]{1,0:T(8,128)(2,1)}), bf16[16,256]{1,0:T(8,128)(2,1)}) %reduce-scatter.9.cloned.1.call-update) | async-done | bytes 8208 | tf_op jit(solution)/shard_map/reduce_scatter | solution.py:92
  480.8 1.3 collective-permute-start.5
  482.6 3.9 collective-permute-done.5
  486.8 0.5 copy-done.6
  487.3 0.9 multiply_convert_fusion
  490.4 1.1 fusion.3
  492.3 1.4 copy.461
  493.7 97.3 %reduce-scatter.11.cloned.1.call-done = bf16[16,256]{1,0:T(8,128)(2,1)} async-done(((bf16[512,256]{1,0:T(8,128)(2,1)}), bf16[16,256]{1,0:T(8,128)(2,1)}) %reduce-scatter.11.cloned.1.call-update) | async-done | bytes 8208 | tf_op jit(solution)/shard_map/reduce_scatter | solution.py:92
  591.1 1.3 maximum_bitcast_fusion.1
  (387 shorter events, 16.8 us)
Async XLA Ops:
  38.1 2.6 collective-permute-start
  64.8 5.5 collective-permute-start.1
  95.5 10.5 %collective-permute-start.2 = (bf16[16,256]{1,0:T(8,128)(2,1)S(1)}, bf16[16,256]{1,0:T(8,128)(2,1)S(1)}, u32[]{:S(2)}, u32[]{:S(2)}) collective-permute-start(bf16[16,256]{1,0:T(8,128)(2,1)S(1)} %multiply_convert_fusion.4), channel_id=1, source_target_pairs={{0,32},{32,64},{64,96},{96,128},{128,160},{160,192},{192,224},{224... | collective-permute-start | bytes 24584 | tf_op jit(solution)/shard_map/ppermute | solution.py:15
  100.4 32.0 %all-to-all-start = ((bf16[32,16,256]{2,1,0:T(8,128)(2,1)}), bf16[32,16,256]{2,1,0:T(8,128)(2,1)S(1)}, u32[]{:S(2)}, u32[]{:S(2)}) async-start(bf16[32,16,256]{2,1,0:T(8,128)(2,1)} %stack.383), calls=%async_computation | async-start | bytes 524288 | tf_op jit(solution)/shard_map/all_to_all | solution.py:82
  131.8 7.1 %copy-start = (bf16[1,16,27,512]{3,1,2,0:T(8,128)(2,1)S(1)}, bf16[1,16,27,512]{3,1,2,0:T(8,128)(2,1)}, u32[]{:S(2)}) copy-start(bf16[1,16,27,512]{3,1,2,0:T(8,128)(2,1)} %param.10) | copy-start | bytes 1327108
  133.1 13.5 %all-to-all-start.1 = ((bf16[32,16,256]{2,1,0:T(8,128)(2,1)}), bf16[32,16,256]{2,1,0:T(8,128)(2,1)S(1)}, u32[]{:S(2)}, u32[]{:S(2)}) async-start(bf16[32,16,256]{2,1,0:T(8,128)(2,1)} %stack.413), calls=%async_computation.2 | async-start | bytes 524288 | tf_op jit(solution)/shard_map/all_to_all | solution.py:82
  143.7 8.6 %copy-start.1 = (bf16[432,256]{1,0:T(8,128)(2,1)}, bf16[432,256]{1,0:T(8,128)(2,1)S(1)}, u32[]{:S(2)}) copy-start(bf16[432,256]{1,0:T(8,128)(2,1)S(1)} %reshape.80) | copy-start | bytes 663556
  147.3 12.8 %all-to-all-start.2 = ((bf16[32,16,256]{2,1,0:T(8,128)(2,1)}), bf16[32,16,256]{2,1,0:T(8,128)(2,1)S(1)}, u32[]{:S(2)}, u32[]{:S(2)}) async-start(bf16[32,16,256]{2,1,0:T(8,128)(2,1)} %stack.443), calls=%async_computation.4 | async-start | bytes 524288 | tf_op jit(solution)/shard_map/all_to_all | solution.py:82
  152.3 110.0 %reduce-scatter.5.cloned.1.call-start = ((), (), s32[]{:S(2)}) async-start(), calls=%async_computation.8 | async-start | bytes 270336 | tf_op jit(solution)/shard_map/reduce_scatter | solution.py:92
  160.8 12.8 %all-to-all-start.3 = ((bf16[32,16,256]{2,1,0:T(8,128)(2,1)}), bf16[32,16,256]{2,1,0:T(8,128)(2,1)S(1)}, u32[]{:S(2)}, u32[]{:S(2)}) async-start(bf16[32,16,256]{2,1,0:T(8,128)(2,1)} %stack.473), calls=%async_computation.6 | async-start | bytes 524288 | tf_op jit(solution)/shard_map/all_to_all | solution.py:82
  165.8 206.1 %reduce-scatter.7.cloned.1.call-start = ((), (), s32[]{:S(2)}) async-start(), calls=%async_computation.9 | async-start | bytes 270336 | tf_op jit(solution)/shard_map/reduce_scatter | solution.py:92
  173.9 207.4 %copy-start.3 = (f32[16,27,256]{2,0,1:T(8,128)}, f32[16,27,256]{2,0,1:T(8,128)S(1)}, u32[]{:S(2)}) copy-start(f32[16,27,256]{2,0,1:T(8,128)S(1)} %fusion.645) | copy-start | bytes 1327108
  262.3 5.7 collective-permute-start.3
  263.6 4.5 copy-start.33
  263.6 4.5 copy-start.34
  263.6 4.5 copy-start.35
  263.6 4.5 copy-start.36
  263.7 4.5 copy-start.37
  272.3 208.4 %reduce-scatter.9.cloned.1.call-start = ((), (), s32[]{:S(2)}) async-start(), calls=%async_computation.10 | async-start | bytes 270336 | tf_op jit(solution)/shard_map/reduce_scatter | solution.py:92
  372.0 5.7 collective-permute-start.4
  381.2 209.8 %reduce-scatter.11.cloned.1.call-start = ((), (), s32[]{:S(2)}) async-start(), calls=%async_computation.11 | async-start | bytes 270336 | tf_op jit(solution)/shard_map/reduce_scatter | solution.py:92
  480.8 5.7 collective-permute-start.5
  482.1 4.5 copy-start.7
  482.1 4.5 copy-start.8
  482.1 4.5 copy-start.9
  482.1 4.5 copy-start.10
  482.1 4.5 copy-start.11
  482.1 4.5 copy-start.12
  482.1 4.5 copy-start.13
  482.1 4.5 copy-start.14
  482.2 4.5 copy-start.15
  482.2 4.5 copy-start.16
  482.2 4.5 copy-start.17
  482.2 4.5 copy-start.18
  482.2 4.5 copy-start.19
  482.2 4.5 copy-start.20
  482.2 4.5 copy-start.21
  482.2 4.5 copy-start.22
  482.2 4.5 copy-start.23
  482.2 4.5 copy-start.24
  482.3 4.5 copy-start.25
  482.3 4.5 copy-start.26
  482.3 4.5 copy-start.27
  482.3 4.5 copy-start.28
  482.3 4.5 copy-start.29
  492.3 98.8 %copy-start.50 = (bf16[16,256]{1,0:T(8,128)(2,1)S(1)}, bf16[16,256]{1,0:T(8,128)(2,1)}, u32[]{:S(2)}) copy-start(bf16[16,256]{1,0:T(8,128)(2,1)} %reduce-scatter.5.cloned.1.call-done) | copy-start | bytes 24580
  492.3 98.8 %copy-start.51 = (bf16[16,256]{1,0:T(8,128)(2,1)S(1)}, bf16[16,256]{1,0:T(8,128)(2,1)}, u32[]{:S(2)}) copy-start(bf16[16,256]{1,0:T(8,128)(2,1)} %reduce-scatter.7.cloned.1.call-done) | copy-start | bytes 24580
  492.3 98.8 %copy-start.52 = (bf16[16,256]{1,0:T(8,128)(2,1)S(1)}, bf16[16,256]{1,0:T(8,128)(2,1)}, u32[]{:S(2)}) copy-start(bf16[16,256]{1,0:T(8,128)(2,1)} %reduce-scatter.9.cloned.1.call-done) | copy-start | bytes 24580
  (19 other events, 47.7 us)
Sparse Core Ops, SparseCore 0:
  157.5 104.8 reduce-scatter.4
  272.5 99.4 reduce-scatter.6
  381.4 99.3 reduce-scatter.8
  491.6 99.3 reduce-scatter.10
